TPU v7x, 512 devices: a whole 4x4x16 slice. The times are simulated.
512 devices in a mesh: grp: 16 (over y, x), ctx: 32 (over z, core).
Axes of the slice: x: 4, y: 4, z: 16, core: 2. Of those that a mesh axis runs over, the one named last changes fastest.
Arguments:
- queries: bfloat16 [262144, 1024], P(('grp', 'ctx')), may hold values from -6 to 6
- keys: bfloat16 [262144, 1024], P(('grp', 'ctx')), may hold values from -6 to 6
- values: bfloat16 [262144, 1024], P(('grp', 'ctx')), may hold values from -6 to 6
- level_weights: float32 [13, 8, 262144], P(None, None, ('grp', 'ctx')), may hold values from 0.1 to 1.5
Outputs:
- attended: bfloat16 [262144, 1024], P(('grp', 'ctx'))
All inputs are finite; a program needn't handle non-finite values.
Results may differ from a plain program's by a relative error of at most 0.0095.
Values may be sent and summed in bfloat16 or wider, within the bound.
No kernel may reach another device: no remote copies, remote signals or barrier semaphores. Data moves between devices by JAX's collectives and lax.ppermute only.
A program may use at most 64 MiB of HBM per device.

v0:
```python
import math
import jax
import jax.numpy as jnp
from jax import lax
from jax.sharding import PartitionSpec as P

DK = 128
STRETCH = 64


def from_partner(block, axis, stride):
    count = lax.axis_size(axis)
    route = []
    for low in range(count):
        high = low | 1 << stride
        if high != low and high < count:
            route += [(low, high), (high, low)]
    return lax.ppermute(block, axis, route)


def level_factor(level_num):
    token_count = STRETCH if level_num == 0 else STRETCH * 2 ** (level_num - 1)
    return 1.0 / math.sqrt(DK * token_count)


def local_part(query_matrix, key_matrix, value_matrix, level_rows):
    row_count = query_matrix.shape[0]
    local_bits = (row_count // STRETCH).bit_length() - 1
    position = jnp.arange(row_count, dtype=jnp.int32)
    block_ids = position // STRETCH
    stretch_xor = jnp.bitwise_xor(block_ids[:, None], block_ids[None, :])
    level_ids = jnp.zeros((row_count, row_count), jnp.int32)
    for bit_num in range(local_bits):
        level_ids = level_ids + (stretch_xor >= 2**bit_num).astype(jnp.int32)
    causal = position[:, None] >= position[None, :]
    weight = jnp.zeros((level_rows.shape[1], row_count, row_count), jnp.float32)
    for level_num in range(local_bits + 1):
        picked = jnp.logical_and(level_ids == level_num, causal)
        weight = weight + jnp.where(
            picked[None], (level_rows[level_num] * level_factor(level_num))[:, :, None], 0.0
        )
    scores = jnp.einsum(
        "thk,shk->hts", query_matrix, key_matrix, preferred_element_type=jnp.float32
    )
    weighted = (scores * weight).astype(jnp.bfloat16)
    return jnp.einsum("hts,shv->thv", weighted, value_matrix, preferred_element_type=jnp.float32)


def sibling_weights(piece_rows, self_position, bit_count):
    device_ids = jnp.arange(piece_rows, dtype=jnp.int32)
    columns = []
    for bit_num in range(bit_count):
        own_block = jnp.right_shift(self_position, bit_num)
        member = jnp.logical_and(
            jnp.right_shift(device_ids, bit_num) == own_block - 1, own_block % 2 == 1
        )
        columns.append(member)
    return jnp.stack(columns, axis=1).astype(jnp.bfloat16)


def collect_into(self_position, bit_count, shard_rows):
    selector = sibling_weights(shard_rows.shape[0], self_position, bit_count)
    return jnp.einsum("nl,nhkv->lhkv", selector, shard_rows, preferred_element_type=jnp.float32)


def on_device(queries, keys, values, level_weights):
    row_count = queries.shape[0]
    head_count = level_weights.shape[1]
    head_width = queries.shape[1] // head_count
    query_matrix = queries.reshape(row_count, head_count, head_width)
    key_matrix = keys.reshape(row_count, head_count, head_width)
    value_matrix = values.reshape(row_count, head_count, head_width)
    local_bits = (row_count // STRETCH).bit_length() - 1
    ctx_bits = lax.axis_size("ctx").bit_length() - 1
    grp_bits = lax.axis_size("grp").bit_length() - 1
    ctx_index = lax.axis_index("ctx")
    grp_index = lax.axis_index("grp")
    kv_state = jnp.einsum(
        "pdx,pdo->dxo", key_matrix, value_matrix, preferred_element_type=jnp.float32
    ).astype(jnp.bfloat16)
    siblings = []
    running = kv_state.astype(jnp.float32)
    for bit_num in range(ctx_bits):
        partner = from_partner(running, "ctx", bit_num)
        left_half = jnp.right_shift(ctx_index, bit_num) % 2 == 1
        siblings.append(jnp.where(left_half, partner, 0.0))
        running = running + partner
    group_state = running.astype(jnp.bfloat16)
    summed = collect_into(
        grp_index, grp_bits, lax.all_gather(group_state[None], "grp", axis=0, tiled=True)
    )
    siblings.extend([summed[bit_num] for bit_num in range(grp_bits)])
    attended = local_part(query_matrix, key_matrix, value_matrix, level_weights)
    for bit_num in range(len(siblings)):
        level_num = 1 + local_bits + bit_num
        level_scale = (level_weights[level_num] * level_factor(level_num)).T
        outer_product = jnp.einsum(
            "ryl,ylf->ryf",
            query_matrix,
            siblings[bit_num].astype(jnp.bfloat16),
            preferred_element_type=jnp.float32,
        )
        attended = attended + outer_product * level_scale[:, :, None]
    return attended.reshape(row_count, head_count * head_width).astype(jnp.bfloat16)


def solution(mesh):
    return jax.shard_map(
        on_device,
        mesh=mesh,
        in_specs=(
            P(("grp", "ctx"), None),
            P(("grp", "ctx"), None),
            P(("grp", "ctx"), None),
            P(None, None, ("grp", "ctx")),
        ),
        out_specs=P(("grp", "ctx"), None),
        check_vma=False,
    )
```

profile of v0, /device:TPU:1, one launch (start us, length us, event | category | flops | bytes accessed | tf_op | source)
XLA Modules:
  0.0 256.2 jit_solution(629913876659027636)
XLA Ops:
  6.5 1.6 copy.118
  8.7 8.7 %collective-permute-start = (f32[8,128,128]{2,1,0:T(8,128)S(1)}, f32[8,128,128]{2,1,0:T(8,128)S(1)}, u32[]{:S(2)}, u32[]{:S(2)}) collective-permute-start(f32[8,128,128]{2,1,0:T(8,128)S(1)} %fusion.22), channel_id=1, source_target_pairs={{0,1},{1,0},{2,3},{3,2},{4,5},{5,4},{6,7},{7,6},{8,9},{9,8},{10,11... | collective-permute-start | bytes 1572872 | tf_op jit(solution)/shard_map/ppermute | solution.py:18
  17.4 1.5 collective-permute-done
  19.0 1.9 collective-permute-start.1
  21.0 13.1 %collective-permute-done.1 = f32[8,128,128]{2,1,0:T(8,128)S(1)} collective-permute-done((f32[8,128,128]{2,1,0:T(8,128)S(1)}, f32[8,128,128]{2,1,0:T(8,128)S(1)}, u32[]{:S(2)}, u32[]{:S(2)}) %collective-permute-start.1) | collective-permute-done | bytes 524320 | tf_op jit(solution)/shard_map/ppermute | solution.py:18
  34.1 2.1 collective-permute-start.2
  36.2 25.9 %collective-permute-done.2 = f32[8,128,128]{2,1,0:T(8,128)S(1)} collective-permute-done((f32[8,128,128]{2,1,0:T(8,128)S(1)}, f32[8,128,128]{2,1,0:T(8,128)S(1)}, u32[]{:S(2)}, u32[]{:S(2)}) %collective-permute-start.2) | collective-permute-done | bytes 524320 | tf_op jit(solution)/shard_map/ppermute | solution.py:18
  62.2 3.5 %collective-permute-start.3 = (f32[8,128,128]{2,1,0:T(8,128)S(1)}, f32[8,128,128]{2,1,0:T(8,128)S(1)}, u32[]{:S(2)}, u32[]{:S(2)}) collective-permute-start(f32[8,128,128]{2,1,0:T(8,128)S(1)} %add.150), channel_id=1, source_target_pairs={{0,8},{8,0},{1,9},{9,1},{2,10},{10,2},{3,11},{11,3},{4,12},{12,4},... | collective-permute-start | bytes 1572872 | tf_op jit(solution)/shard_map/ppermute | solution.py:18
  65.7 58.6 %collective-permute-done.3 = f32[8,128,128]{2,1,0:T(8,128)S(1)} collective-permute-done((f32[8,128,128]{2,1,0:T(8,128)S(1)}, f32[8,128,128]{2,1,0:T(8,128)S(1)}, u32[]{:S(2)}, u32[]{:S(2)}) %collective-permute-start.3) | collective-permute-done | bytes 524320 | tf_op jit(solution)/shard_map/ppermute | solution.py:18
  124.3 10.8 %collective-permute-start.4 = (f32[8,128,128]{2,1,0:T(8,128)S(1)}, f32[8,128,128]{2,1,0:T(8,128)S(1)}, u32[]{:S(2)}, u32[]{:S(2)}) collective-permute-start(f32[8,128,128]{2,1,0:T(8,128)S(1)} %add.153), channel_id=1, source_target_pairs={{0,16},{16,0},{1,17},{17,1},{2,18},{18,2},{3,19},{19,3},{4,20},{20... | collective-permute-start | bytes 1572872 | tf_op jit(solution)/shard_map/ppermute | solution.py:18
  135.1 17.5 %collective-permute-done.4 = f32[8,128,128]{2,1,0:T(8,128)S(1)} collective-permute-done((f32[8,128,128]{2,1,0:T(8,128)S(1)}, f32[8,128,128]{2,1,0:T(8,128)S(1)}, u32[]{:S(2)}, u32[]{:S(2)}) %collective-permute-start.4) | collective-permute-done | bytes 524320 | tf_op jit(solution)/shard_map/ppermute | solution.py:18
  152.6 0.8 copy-done.4
  153.5 0.8 add_convert_fusion
  156.2 1.8 fusion.47
  157.9 7.6 %fusion.2 = f32[8,512,128]{1,2,0:T(8,128)} fusion(f32[8,512]{1,0:T(8,128)} %get-tuple-element.16, f32[8,512]{1,0:T(8,128)} %get-tuple-element.17, f32[8,512]{1,0:T(8,128)} %get-tuple-element.18, f32[8,512]{1,0:T(8,128)} %get-tuple-element.19, pred[512,512]{1,0:T(8,128)(4,1)} %get-tuple-element.23, pred[512,512]{1,0:T(8,128)(4,1)} %get-tuple-element.25, ...), kind=kOutput, calls=%fused_computation.3 | convolution fusion | flops 1092616192 | bytes 6356992 | tf_op jit(solution)/shard_map/hts,shv->thv/dot_general | solution.py:46
  165.6 1.6 fusion.40
  167.2 1.9 fusion.38
  169.1 1.9 fusion.36
  170.9 1.9 fusion.34
  172.8 60.0 %all-gather.3.cloned.1.call-done = bf16[128,128,128]{2,1,0:T(8,128)(2,1)} async-done(((bf16[8,128,128]{2,1,0:T(8,128)(2,1)}), bf16[128,128,128]{2,1,0:T(8,128)(2,1)}) %all-gather.3.cloned.1.call-update) | async-done | bytes 4194320 | tf_op jit(solution)/shard_map/all_gather | solution.py:90
  232.8 4.8 %fusion.19 = bf16[4,8,128,128]{3,0,2,1:T(4,128)(2,1)S(1)} fusion(bf16[16,8,128,128]{3,2,1,0:T(8,128)(2,1)} %bitcast.192, pred[16,1]{0,1:T(4,128)(4,1)S(1)} %copy-done.16, pred[16,1]{0,1:T(4,128)(4,1)S(1)} %copy-done.17, pred[16,1]{0,1:T(4,128)(4,1)S(1)} %copy-done.18, pred[16,1]{0,1:T(4,128)(4,1)S(1)} %copy-done.19), kind=kOutput, calls=%fused_computation.31 | convolution fusion | flops 17301696 | bytes 5242944 | tf_op jit(solution)/shard_map/nl,nhkv->lhkv/dot_general | solution.py:63
  237.5 2.2 fusion.99
  243.9 3.2 %fusion.10 = bf16[512,8,128]{0,2,1:T(8,128)(2,1)} fusion(f32[8,128,512]{2,1,0:T(8,128)S(1)} %fusion.25, f32[8,128,512]{2,1,0:T(8,128)S(1)} %fusion.27, f32[8,128,512]{2,1,0:T(8,128)S(1)} %fusion.29, f32[8,128,512]{2,1,0:T(8,128)S(1)} %fusion.31, f32[8,128,512]{2,1,0:T(8,128)S(1)} %copy-done.3, f32[8,128,512]{2,1,0:T(8,128)S(1)} %copy-done.2, ...), kind=kOutput, calls=%fused_computation.11 | convolution fusion | flops 144310272 | bytes 21643264 | tf_op jit(solution)/shard_map/ryl,ylf->ryf/dot_general | solution.py:97
  247.1 2.3 copy.99
  (54 shorter events, 6.7 us)
Async XLA Ops:
  6.5 151.4 %copy-start = (bf16[512,1024]{1,0:T(8,128)(2,1)S(1)}, bf16[512,1024]{1,0:T(8,128)(2,1)}, u32[]{:S(2)}) copy-start(bf16[512,1024]{1,0:T(8,128)(2,1)} %param.4) | copy-start | bytes 3145732
  6.5 1.7 copy-start.14
  6.5 226.2 %all-gather.3.cloned.1.call-start = ((), (), s32[]{:S(2)}) async-start(), calls=%async_computation | async-start | bytes 4456448 | tf_op jit(solution)/shard_map/all_gather | solution.py:90
  8.7 10.3 %collective-permute-start = (f32[8,128,128]{2,1,0:T(8,128)S(1)}, f32[8,128,128]{2,1,0:T(8,128)S(1)}, u32[]{:S(2)}, u32[]{:S(2)}) collective-permute-start(f32[8,128,128]{2,1,0:T(8,128)S(1)} %fusion.22), channel_id=1, source_target_pairs={{0,1},{1,0},{2,3},{3,2},{4,5},{5,4},{6,7},{7,6},{8,9},{9,8},{10,11... | collective-permute-start | bytes 1572872 | tf_op jit(solution)/shard_map/ppermute | solution.py:18
  18.9 2.0 copy-start.6
  19.0 15.0 %collective-permute-start.1 = (f32[8,128,128]{2,1,0:T(8,128)S(1)}, f32[8,128,128]{2,1,0:T(8,128)S(1)}, u32[]{:S(2)}, u32[]{:S(2)}) collective-permute-start(f32[8,128,128]{2,1,0:T(8,128)S(1)} %add.144), channel_id=1, source_target_pairs={{0,2},{2,0},{1,3},{3,1},{4,6},{6,4},{5,7},{7,5},{8,10},{10,8},{9,1... | collective-permute-start | bytes 1572872 | tf_op jit(solution)/shard_map/ppermute | solution.py:18
  34.0 90.3 %copy-start.7 = (f32[8,128,128]{2,1,0:T(8,128)}, f32[8,128,128]{2,1,0:T(8,128)S(1)}, u32[]{:S(2)}) copy-start(f32[8,128,128]{2,1,0:T(8,128)S(1)} %collective-permute-done.1) | copy-start | bytes 1572868
  34.1 121.4 %copy-start.15 = (f32[13,8,512]{2,1,0:T(8,128)S(1)}, f32[13,8,512]{2,1,0:T(8,128)}, u32[]{:S(2)}) copy-start(f32[13,8,512]{2,1,0:T(8,128)} %param.7) | copy-start | bytes 638980
  34.1 28.0 %collective-permute-start.2 = (f32[8,128,128]{2,1,0:T(8,128)S(1)}, f32[8,128,128]{2,1,0:T(8,128)S(1)}, u32[]{:S(2)}, u32[]{:S(2)}) collective-permute-start(f32[8,128,128]{2,1,0:T(8,128)S(1)} %add.147), channel_id=1, source_target_pairs={{0,4},{4,0},{1,5},{5,1},{2,6},{6,2},{3,7},{7,3},{8,12},{12,8},{9,1... | collective-permute-start | bytes 1572872 | tf_op jit(solution)/shard_map/ppermute | solution.py:18
  62.1 90.5 %copy-start.9 = (f32[8,128,128]{2,1,0:T(8,128)}, f32[8,128,128]{2,1,0:T(8,128)S(1)}, u32[]{:S(2)}) copy-start(f32[8,128,128]{2,1,0:T(8,128)S(1)} %collective-permute-done.2) | copy-start | bytes 1572868
  62.2 62.1 %collective-permute-start.3 = (f32[8,128,128]{2,1,0:T(8,128)S(1)}, f32[8,128,128]{2,1,0:T(8,128)S(1)}, u32[]{:S(2)}, u32[]{:S(2)}) collective-permute-start(f32[8,128,128]{2,1,0:T(8,128)S(1)} %add.150), channel_id=1, source_target_pairs={{0,8},{8,0},{1,9},{9,1},{2,10},{10,2},{3,11},{11,3},{4,12},{12,4},... | collective-permute-start | bytes 1572872 | tf_op jit(solution)/shard_map/ppermute | solution.py:18
  124.2 28.4 %copy-start.11 = (f32[8,128,128]{2,1,0:T(8,128)}, f32[8,128,128]{2,1,0:T(8,128)S(1)}, u32[]{:S(2)}) copy-start(f32[8,128,128]{2,1,0:T(8,128)S(1)} %collective-permute-done.3) | copy-start | bytes 1572868
  124.3 28.3 %collective-permute-start.4 = (f32[8,128,128]{2,1,0:T(8,128)S(1)}, f32[8,128,128]{2,1,0:T(8,128)S(1)}, u32[]{:S(2)}, u32[]{:S(2)}) collective-permute-start(f32[8,128,128]{2,1,0:T(8,128)S(1)} %add.153), channel_id=1, source_target_pairs={{0,16},{16,0},{1,17},{17,1},{2,18},{18,2},{3,19},{19,3},{4,20},{20... | collective-permute-start | bytes 1572872 | tf_op jit(solution)/shard_map/ppermute | solution.py:18
  167.2 1.9 copy-start.10
  169.1 1.9 copy-start.12
  170.9 61.8 %copy-start.16 = (pred[16,1]{0,1:T(4,128)(4,1)S(1)}, pred[16,1]{0,1:T(4,128)(4,1)}, u32[]{:S(2)}) copy-start(pred[16,1]{0,1:T(4,128)(4,1)} %get-tuple-element.26) | copy-start | bytes 52
  170.9 61.8 %copy-start.17 = (pred[16,1]{0,1:T(4,128)(4,1)S(1)}, pred[16,1]{0,1:T(4,128)(4,1)}, u32[]{:S(2)}) copy-start(pred[16,1]{0,1:T(4,128)(4,1)} %get-tuple-element.27) | copy-start | bytes 52
  170.9 61.8 %copy-start.18 = (pred[16,1]{0,1:T(4,128)(4,1)S(1)}, pred[16,1]{0,1:T(4,128)(4,1)}, u32[]{:S(2)}) copy-start(pred[16,1]{0,1:T(4,128)(4,1)} %get-tuple-element.28) | copy-start | bytes 52
  170.9 61.8 %copy-start.19 = (pred[16,1]{0,1:T(4,128)(4,1)S(1)}, pred[16,1]{0,1:T(4,128)(4,1)}, u32[]{:S(2)}) copy-start(pred[16,1]{0,1:T(4,128)(4,1)} %get-tuple-element.29) | copy-start | bytes 52
  240.2 1.6 copy-start.13
  240.7 1.8 copy-start.2
  240.7 2.5 copy-start.3
  241.2 2.7 %copy-start.1 = (f32[8,128,512]{2,1,0:T(8,128)S(1)}, f32[8,128,512]{2,1,0:T(8,128)}, u32[]{:S(2)}) copy-start(f32[8,128,512]{2,1,0:T(8,128)} %fusion.38) | copy-start | bytes 6291460
  241.2 2.7 %copy-start.5 = (f32[8,128,128]{2,1,0:T(8,128)S(1)}, f32[8,128,128]{2,1,0:T(8,128)}, u32[]{:S(2)}) copy-start(f32[8,128,128]{2,1,0:T(8,128)} %copy-done.4) | copy-start | bytes 1572868
  (2 other events, 2.4 us)
Sparse Core Ops, SparseCore 0:
  154.4 78.3 all-gather.2
where the time goes:
time: 257 us; the launch traced here: 256 us
  waiting for transfers between devices  177 us (69%)
  starting transfers between devices  27 us (11%)
  matrix products  25.2 us (10%)
  between operations  13.7 us (5%)
  local copies, waits for them, and re-layouts  9.12 us (4%)
  other arithmetic  4.59 us (2%)
    ppermute x5, waiting for transfers between devices, from_partner(): return lax.ppermute(block, axis, route)  117 us
    all_gather x1, waiting for transfers between devices, on_device(): lax.all_gather(group_state[None], 'grp', axis=0, tiled=True)  60 us
    ppermute x5, starting transfers between devices, from_partner(): return lax.ppermute(block, axis, route)  27 us
    dot_general x9, matrix products, on_device(): jnp.einsum('ryl,ylf->ryf', query_matrix, siblings[bit_num].astype(jnp.bfl...  12.3 us
    dot_general x1, matrix products, local_part(): jnp.einsum('hts,shv->thv', weighted, value_matrix, preferred_element_type...  7.63 us
  transfers between devices with their start and end apart: 6, of which 6 were waited for; matrix products, arithmetic and copies ran while one was open for 7% of the time, Pallas kernels for 0%

commit v1 on v0

--- a/solution.py
+++ b/solution.py
@@ -6,6 +6,12 @@
 
 DK = 128
 STRETCH = 64
+
+
+def reach_array(x0):
+    return jnp.concatenate(
+        lax.all_to_all(jnp.stack(lax.axis_size("grp") * [x0]), "grp", 0, 0), axis=0
+    )
 
 
 def from_partner(block, axis, stride):
@@ -86,9 +92,7 @@
         siblings.append(jnp.where(left_half, partner, 0.0))
         running = running + partner
     group_state = running.astype(jnp.bfloat16)
-    summed = collect_into(
-        grp_index, grp_bits, lax.all_gather(group_state[None], "grp", axis=0, tiled=True)
-    )
+    summed = collect_into(grp_index, grp_bits, reach_array(group_state[None]))
     siblings.extend([summed[bit_num] for bit_num in range(grp_bits)])
     attended = local_part(query_matrix, key_matrix, value_matrix, level_weights)
     for bit_num in range(len(siblings)):

time: 257 us -> 247 us (0.961)
  the two profiles are of different devices: /device:TPU:1 before, /device:TPU:96 now
where the time goes in v1:
time: 247 us
  waiting for transfers between devices  171 us (69%)
  starting transfers between devices  34.5 us (14%)
  matrix products  23.9 us (10%)
  local copies, waits for them, and re-layouts  12.8 us (5%)
  other arithmetic  3.82 us (2%)
    ppermute x5, waiting for transfers between devices, from_partner(): return lax.ppermute(block, axis, route)  126 us
    all_to_all x1, waiting for transfers between devices, reach_array(): lax.all_to_all(jnp.stack(lax.axis_size('grp') * [x0]), 'grp', 0, 0)  45.7 us
    ppermute x5, starting transfers between devices, from_partner(): return lax.ppermute(block, axis, route)  27.6 us
    dot_general x9, matrix products, on_device(): jnp.einsum('ryl,ylf->ryf', query_matrix, siblings[bit_num].astype(jnp.bfl...  11.1 us
    dot_general x1, matrix products, local_part(): jnp.einsum('hts,shv->thv', weighted, value_matrix, preferred_element_type...  7.63 us
    all_to_all x1, starting transfers between devices, reach_array(): lax.all_to_all(jnp.stack(lax.axis_size('grp') * [x0]), 'grp', 0, 0)  6.94 us
  transfers between devices with their start and end apart: 6, of which 6 were waited for; matrix products, arithmetic and copies ran while one was open for 7% of the time, Pallas kernels for 0%

profile of v1, /device:TPU:96, one launch (start us, length us, event | category | flops | bytes accessed | tf_op | source)
XLA Modules:
  0.0 246.7 jit_solution(402290822007762026)
XLA Ops:
  0.0 1.6 copy.92
  2.1 1.9 collective-permute-start
  4.1 1.9 collective-permute-done
  6.0 2.0 collective-permute-start.1
  8.1 13.8 %collective-permute-done.1 = f32[8,128,128]{2,1,0:T(8,128)S(1)} collective-permute-done((f32[8,128,128]{2,1,0:T(8,128)S(1)}, f32[8,128,128]{2,1,0:T(8,128)S(1)}, u32[]{:S(2)}, u32[]{:S(2)}) %collective-permute-start.1) | collective-permute-done | bytes 524320 | tf_op jit(solution)/shard_map/ppermute | solution.py:24
  21.9 5.3 %collective-permute-start.2 = (f32[8,128,128]{2,1,0:T(8,128)S(1)}, f32[8,128,128]{2,1,0:T(8,128)S(1)}, u32[]{:S(2)}, u32[]{:S(2)}) collective-permute-start(f32[8,128,128]{2,1,0:T(8,128)S(1)} %add.147), channel_id=1, source_target_pairs={{0,4},{4,0},{1,5},{5,1},{2,6},{6,2},{3,7},{7,3},{8,12},{12,8},{9,1... | collective-permute-start | bytes 1572872 | tf_op jit(solution)/shard_map/ppermute | solution.py:24
  27.2 22.9 %collective-permute-done.2 = f32[8,128,128]{2,1,0:T(8,128)S(1)} collective-permute-done((f32[8,128,128]{2,1,0:T(8,128)S(1)}, f32[8,128,128]{2,1,0:T(8,128)S(1)}, u32[]{:S(2)}, u32[]{:S(2)}) %collective-permute-start.2) | collective-permute-done | bytes 524320 | tf_op jit(solution)/shard_map/ppermute | solution.py:24
  50.2 8.0 %collective-permute-start.3 = (f32[8,128,128]{2,1,0:T(8,128)S(1)}, f32[8,128,128]{2,1,0:T(8,128)S(1)}, u32[]{:S(2)}, u32[]{:S(2)}) collective-permute-start(f32[8,128,128]{2,1,0:T(8,128)S(1)} %add.150), channel_id=1, source_target_pairs={{0,8},{8,0},{1,9},{9,1},{2,10},{10,2},{3,11},{11,3},{4,12},{12,4},... | collective-permute-start | bytes 1572872 | tf_op jit(solution)/shard_map/ppermute | solution.py:24
  58.2 52.4 %collective-permute-done.3 = f32[8,128,128]{2,1,0:T(8,128)S(1)} collective-permute-done((f32[8,128,128]{2,1,0:T(8,128)S(1)}, f32[8,128,128]{2,1,0:T(8,128)S(1)}, u32[]{:S(2)}, u32[]{:S(2)}) %collective-permute-start.3) | collective-permute-done | bytes 524320 | tf_op jit(solution)/shard_map/ppermute | solution.py:24
  110.6 10.4 %collective-permute-start.4 = (f32[8,128,128]{2,1,0:T(8,128)S(1)}, f32[8,128,128]{2,1,0:T(8,128)S(1)}, u32[]{:S(2)}, u32[]{:S(2)}) collective-permute-start(f32[8,128,128]{2,1,0:T(8,128)S(1)} %add.153), channel_id=1, source_target_pairs={{0,16},{16,0},{1,17},{17,1},{2,18},{18,2},{3,19},{19,3},{4,20},{20... | collective-permute-start | bytes 1572872 | tf_op jit(solution)/shard_map/ppermute | solution.py:24
  121.0 34.7 %collective-permute-done.4 = f32[8,128,128]{2,1,0:T(8,128)S(1)} collective-permute-done((f32[8,128,128]{2,1,0:T(8,128)S(1)}, f32[8,128,128]{2,1,0:T(8,128)S(1)}, u32[]{:S(2)}, u32[]{:S(2)}) %collective-permute-start.4) | collective-permute-done | bytes 524320 | tf_op jit(solution)/shard_map/ppermute | solution.py:24
  155.7 0.8 copy-done.4
  156.6 3.1 %stack.5 = bf16[16,1,8,128,128]{4,3,2,1,0:T(8,128)(2,1)} broadcast(bf16[8,128,128]{2,1,0:T(8,128)(2,1)S(1)} %add_convert_fusion), dimensions={2,3,4} | broadcast | bytes 4456448 | tf_op jit(solution)/shard_map/stack | solution.py:13
  159.6 6.9 %all-to-all-start = ((bf16[16,1,8,128,128]{4,3,2,1,0:T(8,128)(2,1)}), bf16[16,1,8,128,128]{4,3,2,1,0:T(8,128)(2,1)}, u32[]{:S(2)}, u32[]{:S(2)}) async-start(bf16[16,1,8,128,128]{4,3,2,1,0:T(8,128)(2,1)} %stack.5), calls=%async_computation | async-start | bytes 8388608 | tf_op jit(solution)/shard_map/all_to_all | solution.py:13
  168.5 1.7 fusion.48
  170.2 7.6 %fusion.3 = f32[8,512,128]{1,2,0:T(8,128)} fusion(f32[8,512]{1,0:T(8,128)} %get-tuple-element.16, f32[8,512]{1,0:T(8,128)} %get-tuple-element.17, f32[8,512]{1,0:T(8,128)} %get-tuple-element.18, f32[8,512]{1,0:T(8,128)} %get-tuple-element.19, pred[512,512]{1,0:T(8,128)(4,1)} %get-tuple-element.23, pred[512,512]{1,0:T(8,128)(4,1)} %get-tuple-element.25, ...), kind=kOutput, calls=%fused_computation.4 | convolution fusion | flops 1092616192 | bytes 6356992 | tf_op jit(solution)/shard_map/hts,shv->thv/dot_general | solution.py:52
  178.9 1.8 fusion.39
  180.7 1.8 fusion.37
  182.5 1.8 fusion.35
  184.3 45.7 %all-to-all-done = bf16[16,1,8,128,128]{4,3,2,1,0:T(8,128)(2,1)} async-done(((bf16[16,1,8,128,128]{4,3,2,1,0:T(8,128)(2,1)}), bf16[16,1,8,128,128]{4,3,2,1,0:T(8,128)(2,1)}, u32[]{:S(2)}, u32[]{:S(2)}) %all-to-all-start) | async-done | bytes 4194336 | tf_op jit(solution)/shard_map/all_to_all | solution.py:13
  230.0 4.8 %fusion.20 = bf16[4,8,128,128]{3,0,2,1:T(4,128)(2,1)S(1)} fusion(bf16[16,1,8,128,128]{4,3,2,1,0:T(8,128)(2,1)} %all-to-all-done, pred[16,1]{0,1:T(4,128)(4,1)S(1)} %copy-done.16, pred[16,1]{0,1:T(4,128)(4,1)S(1)} %copy-done.17, pred[16,1]{0,1:T(4,128)(4,1)S(1)} %copy-done.18, pred[16,1]{0,1:T(4,128)(4,1)S(1)} %copy-done.19), kind=kOutput, calls=%fused_computation.32 | convolution fusion | flops 17301696 | bytes 5242944 | tf_op jit(solution)/shard_map/nl,nhkv->lhkv/dot_general | solution.py:69
  234.8 2.2 fusion.100
  241.2 3.2 %fusion.11 = bf16[512,8,128]{0,2,1:T(8,128)(2,1)} fusion(f32[8,128,512]{2,1,0:T(8,128)S(1)} %fusion.26, f32[8,128,512]{2,1,0:T(8,128)S(1)} %fusion.28, f32[8,128,512]{2,1,0:T(8,128)S(1)} %fusion.30, f32[8,128,512]{2,1,0:T(8,128)S(1)} %fusion.32, f32[8,128,512]{2,1,0:T(8,128)S(1)} %copy-done.3, f32[8,128,512]{2,1,0:T(8,128)S(1)} %copy-done.2, ...), kind=kOutput, calls=%fused_computation.12 | convolution fusion | flops 144310272 | bytes 21643264 | tf_op jit(solution)/shard_map/ryl,ylf->ryf/dot_general | solution.py:101
  244.4 2.3 copy.73
  (54 shorter events, 7.8 us)
Async XLA Ops:
  0.0 170.2 %copy-start = (bf16[512,1024]{1,0:T(8,128)(2,1)S(1)}, bf16[512,1024]{1,0:T(8,128)(2,1)}, u32[]{:S(2)}) copy-start(bf16[512,1024]{1,0:T(8,128)(2,1)} %param.4) | copy-start | bytes 3145732
  0.0 1.7 copy-start.14
  2.1 3.8 %collective-permute-start = (f32[8,128,128]{2,1,0:T(8,128)S(1)}, f32[8,128,128]{2,1,0:T(8,128)S(1)}, u32[]{:S(2)}, u32[]{:S(2)}) collective-permute-start(f32[8,128,128]{2,1,0:T(8,128)S(1)} %fusion.23), channel_id=1, source_target_pairs={{0,1},{1,0},{2,3},{3,2},{4,5},{5,4},{6,7},{7,6},{8,9},{9,8},{10,11... | collective-permute-start | bytes 1572872 | tf_op jit(solution)/shard_map/ppermute | solution.py:24
  5.9 2.1 copy-start.6
  6.0 15.9 %collective-permute-start.1 = (f32[8,128,128]{2,1,0:T(8,128)S(1)}, f32[8,128,128]{2,1,0:T(8,128)S(1)}, u32[]{:S(2)}, u32[]{:S(2)}) collective-permute-start(f32[8,128,128]{2,1,0:T(8,128)S(1)} %add.144), channel_id=1, source_target_pairs={{0,2},{2,0},{1,3},{3,1},{4,6},{6,4},{5,7},{7,5},{8,10},{10,8},{9,1... | collective-permute-start | bytes 1572872 | tf_op jit(solution)/shard_map/ppermute | solution.py:24
  21.9 88.7 %copy-start.7 = (f32[8,128,128]{2,1,0:T(8,128)}, f32[8,128,128]{2,1,0:T(8,128)S(1)}, u32[]{:S(2)}) copy-start(f32[8,128,128]{2,1,0:T(8,128)S(1)} %collective-permute-done.1) | copy-start | bytes 1572868
  21.9 28.2 %collective-permute-start.2 = (f32[8,128,128]{2,1,0:T(8,128)S(1)}, f32[8,128,128]{2,1,0:T(8,128)S(1)}, u32[]{:S(2)}, u32[]{:S(2)}) collective-permute-start(f32[8,128,128]{2,1,0:T(8,128)S(1)} %add.147), channel_id=1, source_target_pairs={{0,4},{4,0},{1,5},{5,1},{2,6},{6,2},{3,7},{7,3},{8,12},{12,8},{9,1... | collective-permute-start | bytes 1572872 | tf_op jit(solution)/shard_map/ppermute | solution.py:24
  50.1 105.6 %copy-start.9 = (f32[8,128,128]{2,1,0:T(8,128)}, f32[8,128,128]{2,1,0:T(8,128)S(1)}, u32[]{:S(2)}) copy-start(f32[8,128,128]{2,1,0:T(8,128)S(1)} %collective-permute-done.2) | copy-start | bytes 1572868
  50.2 60.4 %collective-permute-start.3 = (f32[8,128,128]{2,1,0:T(8,128)S(1)}, f32[8,128,128]{2,1,0:T(8,128)S(1)}, u32[]{:S(2)}, u32[]{:S(2)}) collective-permute-start(f32[8,128,128]{2,1,0:T(8,128)S(1)} %add.150), channel_id=1, source_target_pairs={{0,8},{8,0},{1,9},{9,1},{2,10},{10,2},{3,11},{11,3},{4,12},{12,4},... | collective-permute-start | bytes 1572872 | tf_op jit(solution)/shard_map/ppermute | solution.py:24
  110.5 45.2 %copy-start.11 = (f32[8,128,128]{2,1,0:T(8,128)}, f32[8,128,128]{2,1,0:T(8,128)S(1)}, u32[]{:S(2)}) copy-start(f32[8,128,128]{2,1,0:T(8,128)S(1)} %collective-permute-done.3) | copy-start | bytes 1572868
  110.6 45.1 %collective-permute-start.4 = (f32[8,128,128]{2,1,0:T(8,128)S(1)}, f32[8,128,128]{2,1,0:T(8,128)S(1)}, u32[]{:S(2)}, u32[]{:S(2)}) collective-permute-start(f32[8,128,128]{2,1,0:T(8,128)S(1)} %add.153), channel_id=1, source_target_pairs={{0,16},{16,0},{1,17},{17,1},{2,18},{18,2},{3,19},{19,3},{4,20},{20... | collective-permute-start | bytes 1572872 | tf_op jit(solution)/shard_map/ppermute | solution.py:24
  159.6 8.2 %copy-start.15 = (f32[13,8,512]{2,1,0:T(8,128)S(1)}, f32[13,8,512]{2,1,0:T(8,128)}, u32[]{:S(2)}) copy-start(f32[13,8,512]{2,1,0:T(8,128)} %param.7) | copy-start | bytes 638980
  159.6 70.4 %all-to-all-start = ((bf16[16,1,8,128,128]{4,3,2,1,0:T(8,128)(2,1)}), bf16[16,1,8,128,128]{4,3,2,1,0:T(8,128)(2,1)}, u32[]{:S(2)}, u32[]{:S(2)}) async-start(bf16[16,1,8,128,128]{4,3,2,1,0:T(8,128)(2,1)} %stack.5), calls=%async_computation | async-start | bytes 8388608 | tf_op jit(solution)/shard_map/all_to_all | solution.py:13
  178.9 1.8 copy-start.10
  180.7 1.8 copy-start.12
  182.5 47.5 %copy-start.16 = (pred[16,1]{0,1:T(4,128)(4,1)S(1)}, pred[16,1]{0,1:T(4,128)(4,1)}, u32[]{:S(2)}) copy-start(pred[16,1]{0,1:T(4,128)(4,1)} %get-tuple-element.26) | copy-start | bytes 52
  182.5 47.5 %copy-start.17 = (pred[16,1]{0,1:T(4,128)(4,1)S(1)}, pred[16,1]{0,1:T(4,128)(4,1)}, u32[]{:S(2)}) copy-start(pred[16,1]{0,1:T(4,128)(4,1)} %get-tuple-element.27) | copy-start | bytes 52
  182.5 47.5 %copy-start.18 = (pred[16,1]{0,1:T(4,128)(4,1)S(1)}, pred[16,1]{0,1:T(4,128)(4,1)}, u32[]{:S(2)}) copy-start(pred[16,1]{0,1:T(4,128)(4,1)} %get-tuple-element.28) | copy-start | bytes 52
  182.5 47.5 %copy-start.19 = (pred[16,1]{0,1:T(4,128)(4,1)S(1)}, pred[16,1]{0,1:T(4,128)(4,1)}, u32[]{:S(2)}) copy-start(pred[16,1]{0,1:T(4,128)(4,1)} %get-tuple-element.29) | copy-start | bytes 52
  237.5 1.6 copy-start.13
  238.0 1.8 copy-start.2
  238.0 2.5 %copy-start.3 = (f32[8,128,512]{2,1,0:T(8,128)S(1)}, f32[8,128,512]{2,1,0:T(8,128)}, u32[]{:S(2)}) copy-start(f32[8,128,512]{2,1,0:T(8,128)} %fusion.35) | copy-start | bytes 6291460
  238.5 2.7 %copy-start.1 = (f32[8,128,512]{2,1,0:T(8,128)S(1)}, f32[8,128,512]{2,1,0:T(8,128)}, u32[]{:S(2)}) copy-start(f32[8,128,512]{2,1,0:T(8,128)} %fusion.39) | copy-start | bytes 6291460
  238.5 2.7 %copy-start.5 = (f32[8,128,128]{2,1,0:T(8,128)S(1)}, f32[8,128,128]{2,1,0:T(8,128)}, u32[]{:S(2)}) copy-start(f32[8,128,128]{2,1,0:T(8,128)} %copy-done.4) | copy-start | bytes 1572868
  (2 other events, 1.9 us)
